TPU v7x, 32 devices: a whole 2x2x4 slice. The times are simulated.
32 devices in a mesh: hel: 4 (over y, core), rad: 8 (over z, x).
Axes of the slice: x: 2, y: 2, z: 4, core: 2. Of those that a mesh axis runs over, the one named last changes fastest.
Arguments:
- older_packet: float32 [4, 512, 8, 1024], P('hel', 'rad'), may hold values from -6 to 6
- newer_packet: float32 [4, 512, 8, 1024], P('hel', 'rad'), may hold values from -6 to 6
- kinetic: bfloat16 [512, 512], replicated, may hold values from -1 to 1, as said below
- transform: bfloat16 [4, 1024, 1024], P('hel'), may hold values from -0.1875 to 0.1875
- potential: bfloat16 [512, 8, 1024], P('rad'), may hold values from -2 to 2
- coupling: bfloat16 [4, 1024], P('hel'), may hold values from 0.29882812 to 1.5
- radial_weight: float32 [512], replicated, may hold values from 0.3 to 2
- damping: float32 [512], P('rad'), may hold values from 0.6 to 1
Outputs:
- older_out: float32 [4, 512, 8, 1024], P('hel', 'rad')
- newer_out: float32 [4, 512, 8, 1024], P('hel', 'rad')
Inputs may be any that keep to these rules, and one draw needn't show every extreme that they name: kinetic is symmetric.
All inputs are finite; a program needn't handle non-finite values.
Results may differ from a plain program's by a relative error of at most 0.014.
Values may be sent and summed in bfloat16 or wider, within the bound.
A program may use at most 64 MiB of HBM per device.

v0:
```python
import jax
import jax.numpy as jnp
from jax import lax
from jax.sharding import PartitionSpec as P

STEPS = 3


SCALE_FACTOR = 0.35


def from_behind(array, axis, by):
    devices = lax.axis_size(axis)
    pairs = [(i, i + by) for i in range(devices) if 0 <= i + by < devices]
    return lax.ppermute(array, axis, pairs)


def coriolis_term(block, coefs, weights):
    lower_block, lower_coefs = from_behind((block, coefs), "hel", 1)
    upper_block = from_behind(block, "hel", -1)
    below = jnp.concatenate([lower_block, block[:-1]], axis=0).astype(jnp.float32)
    below_coefs = jnp.concatenate([lower_coefs, coefs[:-1]], axis=0).astype(jnp.float32)
    above = jnp.concatenate([block[1:], upper_block], axis=0).astype(jnp.float32)
    mixed = below_coefs[:, None, :] * below + coefs.astype(jnp.float32)[:, None, :] * above
    return weights[None, :, None] * mixed


def body(
    older_packet, newer_packet, kinetic, transform, potential, coupling, radial_weight, damping
):
    hel_rows, rad_rows, vib_count, ang_count = newer_packet.shape
    flat_width = vib_count * ang_count
    rank = lax.axis_index("rad")
    previous = older_packet.reshape(hel_rows, rad_rows, flat_width)
    current = newer_packet.reshape(hel_rows, rad_rows, flat_width)
    potential_flat = potential.astype(jnp.float32).reshape(1, rad_rows * vib_count, ang_count)
    tiled_coefs = jnp.tile(coupling, (1, vib_count))
    damp = damping[None, :, None]
    for _ in range(STEPS):
        rounded = current.astype(jnp.bfloat16)
        regrouped = lax.all_to_all(rounded, "rad", split_axis=2, concat_axis=1, tiled=True)
        kinetic_term = jnp.einsum(
            "rs,ksc->krc", kinetic, regrouped, preferred_element_type=jnp.float32
        )
        returned = lax.all_to_all(kinetic_term, "rad", split_axis=1, concat_axis=2, tiled=True)
        start = rank * rad_rows
        local_weights = lax.dynamic_slice_in_dim(radial_weight, start, rad_rows, 0)
        summed = returned + coriolis_term(rounded, tiled_coefs, local_weights)
        off_grid = summed.astype(jnp.bfloat16).astype(jnp.float32)
        angular_rows = rounded.reshape(hel_rows, rad_rows * vib_count, ang_count)
        grid = jnp.einsum(
            "kna,kag->kng", angular_rows, transform, preferred_element_type=jnp.float32
        )
        grid_values = (grid * potential_flat).astype(jnp.bfloat16)
        angular_part = jnp.einsum(
            "kng,kag->kna", grid_values, transform, preferred_element_type=jnp.float32
        )
        applied = SCALE_FACTOR * (off_grid + angular_part.reshape(hel_rows, rad_rows, flat_width))
        following = damp * (2.0 * applied - damp * previous)
        previous = current
        current = following
    shape = (hel_rows, rad_rows, vib_count, ang_count)
    return (previous.reshape(shape), current.reshape(shape))


def solution(mesh):
    return jax.shard_map(
        body,
        mesh=mesh,
        in_specs=(
            P("hel", "rad", None, None),
            P("hel", "rad", None, None),
            P(),
            P("hel", None, None),
            P("rad", None, None),
            P("hel", None),
            P(),
            P("rad"),
        ),
        out_specs=(P("hel", "rad", None, None), P("hel", "rad", None, None)),
        check_vma=False,
    )
```

profile of v0, /device:TPU:0, one launch (start us, length us, event | category | flops | bytes accessed | tf_op | source)
XLA Modules:
  0.0 531.7 jit_solution(2923640305406667698)
XLA Ops:
  5.2 6.8 %copy.40 = bf16[1,64,8192]{1,0,2:T(2,128)(2,1)} copy(bf16[1,64,8192]{2,1,0:T(8,128)(2,1)S(1)} %convert_element_type.91) | data formatting | bytes 2097152 | tf_op jit(solution)/shard_map/convert_element_type | solution.py:40
  12.6 46.5 %reduce.1 = bf16[8192,64]{1,0:T(8,128)(2,1)} reduce(bf16[8192,1,64]{2,1,0:T(2,128)(2,1)} %bitcast.131, bf16[]{:T(256)} %broadcast.50), dimensions={1}, to_apply=%bitcast.113.reduce_sub_computation | reduce | bytes 2097154
  59.1 4.3 reshape.210
  63.4 33.1 %all_to_all.99 = bf16[8,2,32768]{2,1,0:T(2,128)(2,1)} all-to-all(bf16[8,2,32768]{2,1,0:T(2,128)(2,1)} %reshape.210), channel_id=1, replica_groups=mesh['hel'=4,'rad'=8] {'rad'}, dimensions={0} | all-to-all | bytes 2097152 | tf_op jit(solution)/shard_map/all_to_all | solution.py:41
  96.6 6.5 %reshape.211 = bf16[8192,1,64]{2,1,0:T(2,128)(2,1)} reshape(bf16[8,2,32768]{2,1,0:T(2,128)(2,1)} %all_to_all.99) | data formatting | bytes 2097152
  103.1 8.9 %copy.41 = bf16[1,64,8192]{2,1,0:T(8,128)(2,1)} copy(bf16[1,64,8192]{1,0,2:T(2,128)(2,1)} %bitcast.132) | data formatting | bytes 2097152 | tf_op jit(solution)/shard_map/all_to_all | solution.py:41
  116.9 6.1 %copy.43 = f32[1,512,1024]{2,0,1:T(1,128)} copy(f32[1,512,1024]{1,2,0:T(8,128)} %convolution_bitcast_fusion.2) | data formatting | bytes 4194304 | tf_op jit(solution)/shard_map/rs,ksc->krc/transpose | solution.py:42
  123.0 4.5 all-to-all-start.1
  131.2 4.2 collective-permute-start
  135.4 5.5 %fusion.11 = f32[512,1024]{1,0:T(8,128)} fusion(bf16[1,1024,1024]{2,1,0:T(8,128)(2,1)S(1)} %copy-done, bf16[64,8,1024]{2,1,0:T(8,128)(2,1)} %param.12, f32[1,64,8,1024]{3,2,1,0:T(8,128)} %param.9), kind=kOutput, calls=%fused_computation.14 | convolution fusion | flops 2149580800 | bytes 7340032 | tf_op jit(solution)/shard_map/kng,kag->kna/dot_general | solution.py:55
  147.3 27.5 %all-to-all-done.1 = f32[1,512,1024]{2,0,1:T(1,128)} async-done(((f32[1,512,1024]{2,0,1:T(1,128)}), f32[1,512,1024]{2,0,1:T(1,128)}, u32[]{:S(2)}, u32[]{:S(2)}) %all-to-all-start.1) | async-done | bytes 2097184 | tf_op jit(solution)/shard_map/all_to_all | solution.py:45
  182.9 6.8 %copy.45 = bf16[1,64,8192]{1,0,2:T(2,128)(2,1)} copy(bf16[1,64,8192]{2,1,0:T(8,128)(2,1)S(1)} %get-tuple-element.4) | data formatting | bytes 2097152 | tf_op jit(solution)/shard_map/convert_element_type | solution.py:40
  189.7 46.5 %reduce.2 = bf16[8192,64]{1,0:T(8,128)(2,1)} reduce(bf16[8192,1,64]{2,1,0:T(2,128)(2,1)} %bitcast.136, bf16[]{:T(256)} %broadcast.50), dimensions={1}, to_apply=%bitcast.115.reduce_sub_computation | reduce | bytes 2097154
  236.2 4.3 reshape.212
  240.5 29.9 %all_to_all.100 = bf16[8,2,32768]{2,1,0:T(2,128)(2,1)} all-to-all(bf16[8,2,32768]{2,1,0:T(2,128)(2,1)} %reshape.212), channel_id=1, replica_groups=mesh['hel'=4,'rad'=8] {'rad'}, dimensions={0} | all-to-all | bytes 2097152 | tf_op jit(solution)/shard_map/all_to_all | solution.py:41
  270.4 6.5 %reshape.213 = bf16[8192,1,64]{2,1,0:T(2,128)(2,1)} reshape(bf16[8,2,32768]{2,1,0:T(2,128)(2,1)} %all_to_all.100) | data formatting | bytes 2097152
  276.9 8.9 %copy.46 = bf16[1,64,8192]{2,1,0:T(8,128)(2,1)} copy(bf16[1,64,8192]{1,0,2:T(2,128)(2,1)} %bitcast.133) | data formatting | bytes 2097152 | tf_op jit(solution)/shard_map/all_to_all | solution.py:41
  290.7 6.1 %copy.48 = f32[1,512,1024]{2,0,1:T(1,128)} copy(f32[1,512,1024]{1,2,0:T(8,128)} %convolution_bitcast_fusion.1) | data formatting | bytes 4194304 | tf_op jit(solution)/shard_map/rs,ksc->krc/transpose | solution.py:42
  296.8 4.3 all-to-all-start.3
  306.0 5.2 fusion.7
  314.0 34.5 %all-to-all-done.3 = f32[1,512,1024]{2,0,1:T(1,128)} async-done(((f32[1,512,1024]{2,0,1:T(1,128)}), f32[1,512,1024]{2,0,1:T(1,128)}, u32[]{:S(2)}, u32[]{:S(2)}) %all-to-all-start.3) | async-done | bytes 2097184 | tf_op jit(solution)/shard_map/all_to_all | solution.py:45
  356.6 6.8 %copy.50 = bf16[1,64,8192]{1,0,2:T(2,128)(2,1)} copy(bf16[1,64,8192]{2,1,0:T(8,128)(2,1)S(1)} %get-tuple-element.2) | data formatting | bytes 2097152 | tf_op jit(solution)/shard_map/convert_element_type | solution.py:40
  363.4 46.5 %reduce.3 = bf16[8192,64]{1,0:T(8,128)(2,1)} reduce(bf16[8192,1,64]{2,1,0:T(2,128)(2,1)} %bitcast.134, bf16[]{:T(256)} %broadcast.50), dimensions={1}, to_apply=%bitcast.117.reduce_sub_computation | reduce | bytes 2097154
  409.9 4.3 reshape.214
  414.2 29.9 %all_to_all.101 = bf16[8,2,32768]{2,1,0:T(2,128)(2,1)} all-to-all(bf16[8,2,32768]{2,1,0:T(2,128)(2,1)} %reshape.214), channel_id=1, replica_groups=mesh['hel'=4,'rad'=8] {'rad'}, dimensions={0} | all-to-all | bytes 2097152 | tf_op jit(solution)/shard_map/all_to_all | solution.py:41
  444.1 6.5 %reshape.215 = bf16[8192,1,64]{2,1,0:T(2,128)(2,1)} reshape(bf16[8,2,32768]{2,1,0:T(2,128)(2,1)} %all_to_all.101) | data formatting | bytes 2097152
  450.6 8.9 %copy.51 = bf16[1,64,8192]{2,1,0:T(8,128)(2,1)} copy(bf16[1,64,8192]{1,0,2:T(2,128)(2,1)} %bitcast.135) | data formatting | bytes 2097152 | tf_op jit(solution)/shard_map/all_to_all | solution.py:41
  464.4 6.1 %copy.53 = f32[1,512,1024]{2,0,1:T(1,128)} copy(f32[1,512,1024]{1,2,0:T(8,128)} %convolution_bitcast_fusion) | data formatting | bytes 4194304 | tf_op jit(solution)/shard_map/rs,ksc->krc/transpose | solution.py:42
  470.6 4.3 all-to-all-start.5
  479.8 5.2 fusion.3
  487.7 4.2 copy.65
  491.9 30.3 %all-to-all-done.5 = f32[1,512,1024]{2,0,1:T(1,128)} async-done(((f32[1,512,1024]{2,0,1:T(1,128)}), f32[1,512,1024]{2,0,1:T(1,128)}, u32[]{:S(2)}, u32[]{:S(2)}) %all-to-all-start.5) | async-done | bytes 2097184 | tf_op jit(solution)/shard_map/all_to_all | solution.py:45
  (76 shorter events, 70.4 us)
Async XLA Ops:
  0.6 134.8 %copy-start = (bf16[1,1024,1024]{2,1,0:T(8,128)(2,1)S(1)}, bf16[1,1024,1024]{2,1,0:T(8,128)(2,1)}, u32[]{:S(2)}) copy-start(bf16[1,1024,1024]{2,1,0:T(8,128)(2,1)} %param.11) | copy-start | bytes 6291460
  113.8 1.0 copy-start.7
  123.0 8.1 %copy-start.11 = (bf16[1,1024]{1,0:T(2,128)(2,1)S(1)}, bf16[1,1024]{1,0:T(2,128)(2,1)}, u32[]{:S(2)}) copy-start(bf16[1,1024]{1,0:T(2,128)(2,1)} %param.13) | copy-start | bytes 6148
  123.0 51.8 %all-to-all-start.1 = ((f32[1,512,1024]{2,0,1:T(1,128)}), f32[1,512,1024]{2,0,1:T(1,128)}, u32[]{:S(2)}, u32[]{:S(2)}) async-start(f32[1,512,1024]{2,0,1:T(1,128)} %copy.43), calls=%async_computation.1 | async-start | bytes 4194304 | tf_op jit(solution)/shard_map/all_to_all | solution.py:45
  127.5 49.7 %collective-permute-start.1 = (bf16[1,64,8192]{2,1,0:T(8,128)(2,1)S(1)}, bf16[1,64,8192]{2,1,0:T(8,128)(2,1)}, u32[]{:S(2)}, u32[]{:S(2)}) collective-permute-start(bf16[1,64,8192]{2,1,0:T(8,128)(2,1)S(1)} %convert_element_type.91), channel_id=1, source_target_pairs={{0,8},{8,16},{16,24},{1,9},{9,17},{17,25},{2,10},{10,18},{18,26},{... | collective-permute-start | bytes 3145736 | tf_op jit(solution)/shard_map/ppermute | solution.py:15
  129.8 47.4 %collective-permute-start.2 = (bf16[1,64,8192]{2,1,0:T(8,128)(2,1)S(1)}, bf16[1,64,8192]{2,1,0:T(8,128)(2,1)}, u32[]{:S(2)}, u32[]{:S(2)}) collective-permute-start(bf16[1,64,8192]{2,1,0:T(8,128)(2,1)S(1)} %convert_element_type.91), channel_id=1, source_target_pairs={{8,0},{16,8},{24,16},{9,1},{17,9},{25,17},{10,2},{18,10},{26,18},{... | collective-permute-start | bytes 3145736 | tf_op jit(solution)/shard_map/ppermute | solution.py:15
  131.2 16.1 %collective-permute-start = (bf16[1,8192]{1,0:T(2,128)(2,1)S(1)}, bf16[1,8192]{1,0:T(2,128)(2,1)S(1)}, u32[]{:S(2)}, u32[]{:S(2)}) collective-permute-start(bf16[1,8192]{1,0:T(2,128)(2,1)S(1)} %bitcast.162), channel_id=1, source_target_pairs={{0,8},{8,16},{16,24},{1,9},{9,17},{17,25},{2,10},{10,18},{18,26},{... | collective-permute-start | bytes 49160 | tf_op jit(solution)/shard_map/ppermute | solution.py:15
  176.9 1.6 copy-start.2
  176.9 2.2 copy-start.3
  176.9 2.2 copy-start.10
  287.6 1.0 copy-start.8
  296.8 51.7 %all-to-all-start.3 = ((f32[1,512,1024]{2,0,1:T(1,128)}), f32[1,512,1024]{2,0,1:T(1,128)}, u32[]{:S(2)}, u32[]{:S(2)}) async-start(f32[1,512,1024]{2,0,1:T(1,128)} %copy.48), calls=%async_computation.3 | async-start | bytes 4194304 | tf_op jit(solution)/shard_map/all_to_all | solution.py:45
  301.2 49.7 %collective-permute-start.3 = (bf16[1,64,8192]{2,1,0:T(8,128)(2,1)S(1)}, bf16[1,64,8192]{2,1,0:T(8,128)(2,1)}, u32[]{:S(2)}, u32[]{:S(2)}) collective-permute-start(bf16[1,64,8192]{2,1,0:T(8,128)(2,1)S(1)} %get-tuple-element.4), channel_id=1, source_target_pairs={{0,8},{8,16},{16,24},{1,9},{9,17},{17,25},{2,10},{10,18},{18,26},{... | collective-permute-start | bytes 3145736 | tf_op jit(solution)/shard_map/ppermute | solution.py:15
  303.4 47.4 %collective-permute-start.4 = (bf16[1,64,8192]{2,1,0:T(8,128)(2,1)S(1)}, bf16[1,64,8192]{2,1,0:T(8,128)(2,1)}, u32[]{:S(2)}, u32[]{:S(2)}) collective-permute-start(bf16[1,64,8192]{2,1,0:T(8,128)(2,1)S(1)} %get-tuple-element.4), channel_id=1, source_target_pairs={{8,0},{16,8},{24,16},{9,1},{17,9},{25,17},{10,2},{18,10},{26,18},{... | collective-permute-start | bytes 3145736 | tf_op jit(solution)/shard_map/ppermute | solution.py:15
  350.6 1.6 copy-start.1
  350.6 2.2 copy-start.5
  461.3 1.0 copy-start.9
  470.6 51.7 %all-to-all-start.5 = ((f32[1,512,1024]{2,0,1:T(1,128)}), f32[1,512,1024]{2,0,1:T(1,128)}, u32[]{:S(2)}, u32[]{:S(2)}) async-start(f32[1,512,1024]{2,0,1:T(1,128)} %copy.53), calls=%async_computation.5 | async-start | bytes 4194304 | tf_op jit(solution)/shard_map/all_to_all | solution.py:45
  474.9 49.6 %collective-permute-start.5 = (bf16[1,64,8192]{2,1,0:T(8,128)(2,1)S(1)}, bf16[1,64,8192]{2,1,0:T(8,128)(2,1)}, u32[]{:S(2)}, u32[]{:S(2)}) collective-permute-start(bf16[1,64,8192]{2,1,0:T(8,128)(2,1)S(1)} %get-tuple-element.2), channel_id=1, source_target_pairs={{0,8},{8,16},{16,24},{1,9},{9,17},{17,25},{2,10},{10,18},{18,26},{... | collective-permute-start | bytes 3145736 | tf_op jit(solution)/shard_map/ppermute | solution.py:15
  477.2 47.3 %collective-permute-start.6 = (bf16[1,64,8192]{2,1,0:T(8,128)(2,1)S(1)}, bf16[1,64,8192]{2,1,0:T(8,128)(2,1)}, u32[]{:S(2)}, u32[]{:S(2)}) collective-permute-start(bf16[1,64,8192]{2,1,0:T(8,128)(2,1)S(1)} %get-tuple-element.2), channel_id=1, source_target_pairs={{8,0},{16,8},{24,16},{9,1},{17,9},{25,17},{10,2},{18,10},{26,18},{... | collective-permute-start | bytes 3145736 | tf_op jit(solution)/shard_map/ppermute | solution.py:15
  524.3 1.6 copy-start.4
  524.3 2.2 copy-start.6
where the time goes:
time: 542 us; the launch traced here: 532 us
  other arithmetic  151 us (28%)
  local copies, waits for them, and re-layouts  144 us (27%)
  blocking collectives  92.9 us (17%)
  waiting for transfers between devices  92.4 us (17%)
  starting transfers between devices  28.1 us (5%)
  matrix products  22.1 us (4%)
    unnamed x4, other arithmetic  140 us
    all_to_all x3, blocking collectives, body(): lax.all_to_all(rounded, 'rad', split_axis=2, concat_axis=1, tiled=True)  92.9 us
    all_to_all x3, waiting for transfers between devices, body(): lax.all_to_all(kinetic_term, 'rad', split_axis=1, concat_axis=2, tiled=True)  92.4 us
    unnamed x43, local copies, waits for them, and re-layouts  58.5 us
    all_to_all x9, local copies, waits for them, and re-layouts, body(): lax.all_to_all(rounded, 'rad', split_axis=2, concat_axis=1, tiled=True)  28.5 us
    convert_element_type x3, local copies, waits for them, and re-layouts, body(): rounded = current.astype(jnp.bfloat16)  20.3 us
    transpose x3, local copies, waits for them, and re-layouts, body(): jnp.einsum('rs,ksc->krc', kinetic, regrouped, preferred_element_type=jnp....  18.3 us
    dot_general x3, matrix products, body(): jnp.einsum('kng,kag->kna', grid_values, transform, preferred_element_type...  15.9 us
  transfers between devices with their start and end apart: 10, of which 3 were waited for; matrix products, arithmetic and copies ran while one was open for 8% of the time, Pallas kernels for 0%

commit v1 on v0

--- a/solution.py
+++ b/solution.py
@@ -63,9 +63,64 @@
     return (previous.reshape(shape), current.reshape(shape))
 
 
+def by_vibration(
+    older_packet, newer_packet, kinetic, transform, potential, coupling, radial_weight, damping
+):
+    hel_rows, rad_rows, vib_count, ang_count = newer_packet.shape
+    devices = lax.axis_size("rad")
+
+    def scatter(array):
+        return lax.all_to_all(array, "rad", split_axis=2, concat_axis=1, tiled=True)
+
+    rounded = scatter(newer_packet.astype(jnp.bfloat16))
+    previous = scatter(older_packet.astype(jnp.bfloat16)).astype(jnp.float32)
+    pot = scatter(potential[None])[0].astype(jnp.float32)
+    damp = lax.all_gather(damping, "rad", tiled=True)[None, :, None, None]
+    weight = radial_weight[None, :, None, None]
+    current = rounded.astype(jnp.float32)
+    lower_coefs = from_behind(coupling, "hel", 1)
+    coefs = jnp.concatenate([lower_coefs, coupling], axis=0).astype(jnp.float32)
+    coefs = coefs[:, None, None, :]
+    history = []
+    for step in range(STEPS):
+        lower = from_behind(rounded[-1:], "hel", 1)
+        upper = from_behind(rounded[:1], "hel", -1)
+        padded = jnp.concatenate([lower, rounded, upper], axis=0).astype(jnp.float32)
+        mixed = coefs[:-1] * padded[:-2] + coefs[1:] * padded[2:]
+        radial = jnp.einsum(
+            "rs,ksva->krva", kinetic, rounded, preferred_element_type=jnp.float32
+        )
+        off_grid = radial + weight * mixed
+        grid = jnp.einsum(
+            "krva,kag->krvg", rounded, transform, preferred_element_type=jnp.float32
+        )
+        grid_values = (grid * pot[None]).astype(jnp.bfloat16)
+        angular = jnp.einsum(
+            "krvg,kag->krva", grid_values, transform, preferred_element_type=jnp.float32
+        )
+        applied = SCALE_FACTOR * (off_grid + angular)
+        following = damp * (2.0 * applied - damp * previous)
+        previous = current
+        current = following
+        rounded = current.astype(jnp.bfloat16)
+        history.append(rounded)
+
+    def gather(array):
+        back = lax.all_to_all(array, "rad", split_axis=1, concat_axis=2, tiled=True)
+        return back.astype(jnp.float32)
+
+    return gather(history[-2]), gather(history[-1])
+
+
+def whole_body(older_packet, newer_packet, *rest):
+    if newer_packet.shape[2] % lax.axis_size("rad") == 0:
+        return by_vibration(older_packet, newer_packet, *rest)
+    return body(older_packet, newer_packet, *rest)
+
+
 def solution(mesh):
     return jax.shard_map(
-        body,
+        whole_body,
         mesh=mesh,
         in_specs=(
             P("hel", "rad", None, None),

time: 542 us -> 240 us (0.44)
  the two profiles are of different devices: /device:TPU:0 before, /device:TPU:1 now
where the time goes in v1:
time: 240 us; the launch traced here: 239 us
  waiting for transfers between devices  69.2 us (29%)
  starting transfers between devices  54.2 us (23%)
  local copies, waits for them, and re-layouts  49.3 us (21%)
  blocking collectives  22.2 us (9%)
  matrix products  21.9 us (9%)
  other arithmetic  20.4 us (8%)
    all_to_all x3, waiting for transfers between devices, scatter(): return lax.all_to_all(array, 'rad', split_axis=2, concat_axis=1, tiled=True)  43.6 us
    unnamed x41, local copies, waits for them, and re-layouts  31.3 us
    ppermute x7, starting transfers between devices, from_behind(): return lax.ppermute(array, axis, pairs)  27.4 us
    unnamed x1, blocking collectives  22.2 us
    unnamed x2, other arithmetic  17.1 us
    ppermute x7, waiting for transfers between devices, from_behind(): return lax.ppermute(array, axis, pairs)  15.9 us
    all_to_all x3, starting transfers between devices, scatter(): return lax.all_to_all(array, 'rad', split_axis=2, concat_axis=1, tiled=True)  15.4 us
    all_to_all x2, starting transfers between devices, gather(): back = lax.all_to_all(array, 'rad', split_axis=1, concat_axis=2, tiled=True)  11.5 us
  transfers between devices with their start and end apart: 12, of which 8 were waited for; matrix products, arithmetic and copies ran while one was open for 23% of the time, Pallas kernels for 0%

profile of v1, /device:TPU:1, one launch (start us, length us, event | category | flops | bytes accessed | tf_op | source)
XLA Modules:
  0.0 238.9 jit_solution(4331558418676827421)
XLA Ops:
  0.6 3.8 %copy.57 = bf16[1,64,8,1024]{3,1,0,2:T(8,128)(2,1)} copy(f32[1,64,8,1024]{3,2,1,0:T(8,128)} %param.8) | data formatting | bytes 3145728 | tf_op args[0]
  4.5 6.3 %all-to-all-start.2 = ((bf16[1,64,8,1024]{3,1,0,2:T(8,128)(2,1)}), bf16[1,64,8,1024]{3,1,0,2:T(8,128)(2,1)S(1)}, u32[]{:S(2)}, u32[]{:S(2)}) async-start(bf16[1,64,8,1024]{3,1,0,2:T(8,128)(2,1)} %copy.57), calls=%async_computation.2 | async-start | bytes 2097152 | tf_op jit(solution)/shard_map/all_to_all | solution.py:73
  10.8 3.7 %copy.58 = bf16[1,64,8,1024]{3,1,0,2:T(8,128)(2,1)} copy(f32[1,64,8,1024]{3,2,1,0:T(8,128)} %param.9) | data formatting | bytes 3145728 | tf_op args[1]
  14.5 21.3 %all-to-all-done.2 = bf16[1,64,8,1024]{3,1,0,2:T(8,128)(2,1)S(1)} async-done(((bf16[1,64,8,1024]{3,1,0,2:T(8,128)(2,1)}), bf16[1,64,8,1024]{3,1,0,2:T(8,128)(2,1)S(1)}, u32[]{:S(2)}, u32[]{:S(2)}) %all-to-all-start.2) | async-done | bytes 1048608 | tf_op jit(solution)/shard_map/all_to_all | solution.py:73
  36.7 4.6 %all-to-all-start = ((bf16[1,64,8,1024]{3,1,0,2:T(8,128)(2,1)}), bf16[1,64,8,1024]{3,1,0,2:T(8,128)(2,1)S(1)}, u32[]{:S(2)}, u32[]{:S(2)}) async-start(bf16[1,64,8,1024]{3,1,0,2:T(8,128)(2,1)} %copy.58), calls=%async_computation | async-start | bytes 2097152 | tf_op jit(solution)/shard_map/all_to_all | solution.py:73
  41.4 2.8 %copy.59 = bf16[64,8,1024]{2,0,1:T(8,128)(2,1)} copy(bf16[64,8,1024]{2,1,0:T(8,128)(2,1)} %param.12) | data formatting | bytes 2097152 | tf_op args[4]
  44.1 22.3 %all-to-all-done = bf16[1,64,8,1024]{3,1,0,2:T(8,128)(2,1)S(1)} async-done(((bf16[1,64,8,1024]{3,1,0,2:T(8,128)(2,1)}), bf16[1,64,8,1024]{3,1,0,2:T(8,128)(2,1)S(1)}, u32[]{:S(2)}, u32[]{:S(2)}) %all-to-all-start) | async-done | bytes 1048608 | tf_op jit(solution)/shard_map/all_to_all | solution.py:73
  66.5 4.4 %all-to-all-start.1 = ((bf16[1,64,8,1024]{3,1,0,2:T(8,128)(2,1)}), bf16[1,64,8,1024]{3,1,0,2:T(8,128)(2,1)}, u32[]{:S(2)}, u32[]{:S(2)}) async-start(bf16[1,64,8,1024]{3,1,0,2:T(8,128)(2,1)} %bitcast.126), calls=%async_computation.1 | async-start | bytes 2097152 | tf_op jit(solution)/shard_map/all_to_all | solution.py:73
  70.9 4.4 %collective-permute-start = (bf16[1,1024]{1,0:T(2,128)(2,1)S(1)}, bf16[1,1024]{1,0:T(2,128)(2,1)S(1)}, u32[]{:S(2)}, u32[]{:S(2)}) collective-permute-start(bf16[1,1024]{1,0:T(2,128)(2,1)S(1)} %copy-done.9), channel_id=1, source_target_pairs={{0,8},{8,16},{16,24},{1,9},{9,17},{17,25},{2,10},{10,18},{18,26},{... | collective-permute-start | bytes 6152 | tf_op jit(solution)/shard_map/ppermute | solution.py:15
  76.9 22.2 %all-reduce = f32[512]{0:T(512)S(1)} all-reduce(f32[512]{0:T(512)S(1)} %dynamic-update-slice), channel_id=1, replica_groups=mesh['hel'=4,'rad'=8] {'rad'}, use_global_device_ids=true, to_apply=%add | all-reduce | flops 512 | bytes 4096
  100.4 6.6 %collective-permute-start.2 = (bf16[1,512,1,1024]{1,3,2,0:T(8,128)(2,1)}, bf16[1,512,1,1024]{1,3,2,0:T(8,128)(2,1)}, u32[]{:S(2)}, u32[]{:S(2)}) collective-permute-start(bf16[1,512,1,1024]{1,3,2,0:T(8,128)(2,1)} %copy.33), channel_id=1, source_target_pairs={{8,0},{16,8},{24,16},{9,1},{17,9},{25,17},{10,2},{18,10},{26,18},{... | collective-permute-start | bytes 3145736 | tf_op jit(solution)/shard_map/ppermute | solution.py:15
  107.0 3.0 %collective-permute-start.1 = (bf16[1,512,1,1024]{1,3,2,0:T(8,128)(2,1)}, bf16[1,512,1,1024]{1,3,2,0:T(8,128)(2,1)}, u32[]{:S(2)}, u32[]{:S(2)}) collective-permute-start(bf16[1,512,1,1024]{1,3,2,0:T(8,128)(2,1)} %copy.33), channel_id=1, source_target_pairs={{0,8},{8,16},{16,24},{1,9},{9,17},{17,25},{2,10},{10,18},{18,26},{... | collective-permute-start | bytes 3145736 | tf_op jit(solution)/shard_map/ppermute | solution.py:15
  110.1 2.8 %bitcast_convert_fusion = f32[1,64,8,1,1024]{4,1,2,3,0:T(8,128)} fusion(bf16[1,64,8,1024]{3,1,0,2:T(8,128)(2,1)} %copy-done.1), kind=kLoop, calls=%fused_computation.54 | loop fusion | flops 524288 | bytes 3145728 | tf_op jit(solution)/shard_map/convert_element_type | solution.py:76
  112.9 2.9 %copy.41 = f32[1,512,1,1024]{1,3,2,0:T(8,128)} copy(f32[1,512,1,1024]{3,1,2,0:T(8,128)} %bitcast.123) | data formatting | bytes 4194304 | tf_op jit(solution)/shard_map/convert_element_type | solution.py:76
  115.8 3.1 %fusion.57 = f32[1024,512]{1,0:T(8,128)} fusion(bf16[512,1024]{1,0:T(8,128)(2,1)S(1)} %bitcast.117, bf16[512,512]{1,0:T(8,128)(2,1)} %param.10), kind=kOutput, calls=%fused_computation.65 | convolution fusion | flops 536870912 | bytes 3670016 | tf_op jit(solution)/shard_map/rs,ksva->krva/dot_general | solution.py:90
  118.9 2.6 %fusion.23 = bf16[512,1024]{1,0:T(8,128)(2,1)S(1)} fusion(bf16[1,64,8,1,1024]{4,1,2,3,0:T(8,128)(2,1)} %bitcast.26, bf16[512,1024]{1,0:T(8,128)(2,1)S(1)} %bitcast.118, bf16[1,1024,1024]{2,1,0:T(8,128)(2,1)S(1)} %copy-done), kind=kOutput, calls=%fused_computation.31 | convolution fusion | flops 1075314688 | bytes 5242880 | tf_op jit(solution)/shard_map/krva,kag->krvg/dot_general | solution.py:94
  122.1 4.4 %fusion.54 = (bf16[1,512,1,1024]{1,3,2,0:T(8,128)(2,1)S(1)}, f32[1,512,1,1024]{1,3,2,0:T(8,128)}) fusion(f32[1,512,1,1024]{1,3,2,0:T(8,128)S(1)} %copy-done.3, bf16[1,512,1,1024]{1,3,2,0:T(8,128)(2,1)} %collective-permute-done.2, bf16[1,512,1,1024]{1,3,2,0:T(8,128)(2,1)S(1)} %copy-done.6, bf16[1,512,1,1024]{1,3,2,0:T(8,128)(2,1)} %collective-permute-done.1, ...), kind=kOutput, calls=%fused_computation.63 | convolution fusion | flops 1082654720 | bytes 13643776 | tf_op jit(solution)/shard_map/krvg,kag->krva/dot_general | solution.py:98
  128.4 4.6 %collective-permute-start.3 = (bf16[1,512,1,1024]{1,3,2,0:T(8,128)(2,1)S(1)}, bf16[1,512,1,1024]{1,3,2,0:T(8,128)(2,1)S(1)}, u32[]{:S(2)}, u32[]{:S(2)}) collective-permute-start(bf16[1,512,1,1024]{1,3,2,0:T(8,128)(2,1)S(1)} %get-tuple-element.6), channel_id=1, source_target_pairs={{0,8},{8,16},{16,24},{1,9},{9,17},{17,25},{2,10},{10,18},{18,26},{... | collective-permute-start | bytes 3145736 | tf_op jit(solution)/shard_map/ppermute | solution.py:15
  136.8 6.5 %collective-permute-done.4 = bf16[1,512,1,1024]{1,3,2,0:T(8,128)(2,1)S(1)} collective-permute-done((bf16[1,512,1,1024]{1,3,2,0:T(8,128)(2,1)S(1)}, bf16[1,512,1,1024]{1,3,2,0:T(8,128)(2,1)S(1)}, u32[]{:S(2)}, u32[]{:S(2)}) %collective-permute-start.4) | collective-permute-done | bytes 1048608 | tf_op jit(solution)/shard_map/ppermute | solution.py:15
  146.2 3.9 %copy.44 = bf16[1,512,1,1024]{3,2,0,1:T(2,128)(2,1)} copy(bf16[1,512,1,1024]{1,3,2,0:T(8,128)(2,1)S(1)} %fusion.15) | data formatting | bytes 2097152 | tf_op jit(solution)/shard_map/convert_element_type | solution.py:105
  150.7 8.1 %reduce = bf16[512,1024]{1,0:T(8,128)(2,1)S(1)} reduce(bf16[512,1,1,1024]{3,2,1,0:T(2,128)(2,1)} %bitcast.121, bf16[]{:T(256)} %broadcast.44), dimensions={1,2}, to_apply=%bitcast.99.reduce_sub_computation | reduce | bytes 2097154
  160.4 5.8 %all-to-all-start.3 = ((bf16[8,2,32768]{2,1,0:T(2,128)(2,1)}), bf16[8,2,32768]{2,1,0:T(2,128)(2,1)S(1)}, u32[]{:S(2)}, u32[]{:S(2)}) async-start(bf16[8,2,32768]{2,1,0:T(2,128)(2,1)} %reshape.316), calls=%async_computation.3 | async-start | bytes 2097152 | tf_op jit(solution)/shard_map/all_to_all | solution.py:109
  168.0 4.9 %collective-permute-start.5 = (bf16[1,512,1,1024]{1,3,2,0:T(8,128)(2,1)}, bf16[1,512,1,1024]{1,3,2,0:T(8,128)(2,1)S(1)}, u32[]{:S(2)}, u32[]{:S(2)}) collective-permute-start(bf16[1,512,1,1024]{1,3,2,0:T(8,128)(2,1)} %copy-done.4), channel_id=1, source_target_pairs={{0,8},{8,16},{16,24},{1,9},{9,17},{17,25},{2,10},{10,18},{18,26},{... | collective-permute-start | bytes 3145736 | tf_op jit(solution)/shard_map/ppermute | solution.py:15
  172.9 2.8 %fusion.25 = bf16[512,1024]{1,0:T(8,128)(2,1)S(1)} fusion(bf16[1,64,8,1,1024]{4,1,2,3,0:T(8,128)(2,1)} %bitcast.26, bf16[1,1024,1024]{2,1,0:T(8,128)(2,1)S(1)} %copy-done, bf16[1,512,1,1024]{1,3,2,0:T(8,128)(2,1)} %copy-done.4), kind=kOutput, calls=%fused_computation.33 | convolution fusion | flops 1075314688 | bytes 5242880 | tf_op jit(solution)/shard_map/krva,kag->krvg/dot_general | solution.py:94
  177.1 6.4 %collective-permute-done.6 = bf16[1,512,1,1024]{1,3,2,0:T(8,128)(2,1)S(1)} collective-permute-done((bf16[1,512,1,1024]{1,3,2,0:T(8,128)(2,1)}, bf16[1,512,1,1024]{1,3,2,0:T(8,128)(2,1)S(1)}, u32[]{:S(2)}, u32[]{:S(2)}) %collective-permute-start.6) | collective-permute-done | bytes 1048608 | tf_op jit(solution)/shard_map/ppermute | solution.py:15
  187.1 6.0 %copy.47 = bf16[1,512,1,1024]{3,2,0,1:T(2,128)(2,1)} copy(bf16[1,512,1,1024]{1,3,2,0:T(8,128)(2,1)} %fusion.7) | data formatting | bytes 2097152 | tf_op jit(solution)/shard_map/convert_element_type | solution.py:105
  193.0 9.1 %reduce.1 = bf16[512,1024]{1,0:T(8,128)(2,1)} reduce(bf16[512,1,1,1024]{3,2,1,0:T(2,128)(2,1)} %bitcast.122, bf16[]{:T(256)} %broadcast.44), dimensions={1,2}, to_apply=%bitcast.101.reduce_sub_computation | reduce | bytes 2097154
  202.1 2.6 %reshape.318 = bf16[8,2,32768]{2,1,0:T(2,128)(2,1)} reshape(bf16[512,1024]{1,0:T(8,128)(2,1)} %reduce.1) | data formatting | bytes 2097152
  204.7 5.7 %all-to-all-start.4 = ((bf16[8,2,32768]{2,1,0:T(2,128)(2,1)}), bf16[8,2,32768]{2,1,0:T(2,128)(2,1)}, u32[]{:S(2)}, u32[]{:S(2)}) async-start(bf16[8,2,32768]{2,1,0:T(2,128)(2,1)} %reshape.318), calls=%async_computation.4 | async-start | bytes 2097152 | tf_op jit(solution)/shard_map/all_to_all | solution.py:109
  210.4 3.4 %reshape.317 = bf16[512,1,1,1024]{3,2,1,0:T(2,128)(2,1)} reshape(bf16[8,2,32768]{2,1,0:T(2,128)(2,1)S(1)} %all-to-all-done.3) | data formatting | bytes 2097152
  218.6 9.7 %all-to-all-done.4 = bf16[8,2,32768]{2,1,0:T(2,128)(2,1)} async-done(((bf16[8,2,32768]{2,1,0:T(2,128)(2,1)}), bf16[8,2,32768]{2,1,0:T(2,128)(2,1)}, u32[]{:S(2)}, u32[]{:S(2)}) %all-to-all-start.4) | async-done | bytes 1048608 | tf_op jit(solution)/shard_map/all_to_all | solution.py:109
  228.3 5.8 %reshape.319 = bf16[512,1,1,1024]{3,2,1,0:T(2,128)(2,1)} reshape(bf16[8,2,32768]{2,1,0:T(2,128)(2,1)} %all-to-all-done.4) | data formatting | bytes 2097152
  (56 shorter events, 30.8 us)
Async XLA Ops:
  0.6 118.3 %copy-start = (bf16[1,1024,1024]{2,1,0:T(8,128)(2,1)S(1)}, bf16[1,1024,1024]{2,1,0:T(8,128)(2,1)}, u32[]{:S(2)}) copy-start(bf16[1,1024,1024]{2,1,0:T(8,128)(2,1)} %param.11) | copy-start | bytes 6291460
  4.5 31.3 %all-to-all-start.2 = ((bf16[1,64,8,1024]{3,1,0,2:T(8,128)(2,1)}), bf16[1,64,8,1024]{3,1,0,2:T(8,128)(2,1)S(1)}, u32[]{:S(2)}, u32[]{:S(2)}) async-start(bf16[1,64,8,1024]{3,1,0,2:T(8,128)(2,1)} %copy.57), calls=%async_computation.2 | async-start | bytes 2097152 | tf_op jit(solution)/shard_map/all_to_all | solution.py:73
  35.8 1.0 copy-start.1
  36.7 29.7 %all-to-all-start = ((bf16[1,64,8,1024]{3,1,0,2:T(8,128)(2,1)}), bf16[1,64,8,1024]{3,1,0,2:T(8,128)(2,1)S(1)}, u32[]{:S(2)}, u32[]{:S(2)}) async-start(bf16[1,64,8,1024]{3,1,0,2:T(8,128)(2,1)} %copy.58), calls=%async_computation | async-start | bytes 2097152 | tf_op jit(solution)/shard_map/all_to_all | solution.py:73
  41.3 29.6 %copy-start.9 = (bf16[1,1024]{1,0:T(2,128)(2,1)S(1)}, bf16[1,1024]{1,0:T(2,128)(2,1)}, u32[]{:S(2)}) copy-start(bf16[1,1024]{1,0:T(2,128)(2,1)} %param.13) | copy-start | bytes 6148
  41.3 34.0 %copy-start.12 = (u32[32]{0:T(128)S(1)}, u32[32]{0:T(128)}, u32[]{:S(2)}) copy-start(u32[32]{0:T(128)} %constant.12) | copy-start | bytes 388
  41.3 35.3 %copy-start.11 = (f32[64]{0:T(128)S(1)}, f32[64]{0:T(128)}, u32[]{:S(2)}) copy-start(f32[64]{0:T(128)} %param.15) | copy-start | bytes 772
  66.5 52.4 %all-to-all-start.1 = ((bf16[1,64,8,1024]{3,1,0,2:T(8,128)(2,1)}), bf16[1,64,8,1024]{3,1,0,2:T(8,128)(2,1)}, u32[]{:S(2)}, u32[]{:S(2)}) async-start(bf16[1,64,8,1024]{3,1,0,2:T(8,128)(2,1)} %bitcast.126), calls=%async_computation.1 | async-start | bytes 2097152 | tf_op jit(solution)/shard_map/all_to_all | solution.py:73
  70.9 28.1 %collective-permute-start = (bf16[1,1024]{1,0:T(2,128)(2,1)S(1)}, bf16[1,1024]{1,0:T(2,128)(2,1)S(1)}, u32[]{:S(2)}, u32[]{:S(2)}) collective-permute-start(bf16[1,1024]{1,0:T(2,128)(2,1)S(1)} %copy-done.9), channel_id=1, source_target_pairs={{0,8},{8,16},{16,24},{1,9},{9,17},{17,25},{2,10},{10,18},{18,26},{... | collective-permute-start | bytes 6152 | tf_op jit(solution)/shard_map/ppermute | solution.py:15
  100.4 21.2 %collective-permute-start.2 = (bf16[1,512,1,1024]{1,3,2,0:T(8,128)(2,1)}, bf16[1,512,1,1024]{1,3,2,0:T(8,128)(2,1)}, u32[]{:S(2)}, u32[]{:S(2)}) collective-permute-start(bf16[1,512,1,1024]{1,3,2,0:T(8,128)(2,1)} %copy.33), channel_id=1, source_target_pairs={{8,0},{16,8},{24,16},{9,1},{17,9},{25,17},{10,2},{18,10},{26,18},{... | collective-permute-start | bytes 3145736 | tf_op jit(solution)/shard_map/ppermute | solution.py:15
  107.0 15.1 %collective-permute-start.1 = (bf16[1,512,1,1024]{1,3,2,0:T(8,128)(2,1)}, bf16[1,512,1,1024]{1,3,2,0:T(8,128)(2,1)}, u32[]{:S(2)}, u32[]{:S(2)}) collective-permute-start(bf16[1,512,1,1024]{1,3,2,0:T(8,128)(2,1)} %copy.33), channel_id=1, source_target_pairs={{0,8},{8,16},{16,24},{1,9},{9,17},{17,25},{2,10},{10,18},{18,26},{... | collective-permute-start | bytes 3145736 | tf_op jit(solution)/shard_map/ppermute | solution.py:15
  118.9 3.2 %copy-start.2 = (f32[1024,512]{1,0:T(8,128)S(1)}, f32[1024,512]{1,0:T(8,128)}, u32[]{:S(2)}) copy-start(f32[1024,512]{1,0:T(8,128)} %fusion.57) | copy-start | bytes 6291460
  118.9 3.2 %copy-start.3 = (f32[1,512,1,1024]{1,3,2,0:T(8,128)S(1)}, f32[1,512,1,1024]{1,3,2,0:T(8,128)}, u32[]{:S(2)}) copy-start(f32[1,512,1,1024]{1,3,2,0:T(8,128)} %copy.41) | copy-start | bytes 6291460
  118.9 3.2 %copy-start.6 = (bf16[1,512,1,1024]{1,3,2,0:T(8,128)(2,1)S(1)}, bf16[1,512,1,1024]{1,3,2,0:T(8,128)(2,1)}, u32[]{:S(2)}) copy-start(bf16[1,512,1,1024]{1,3,2,0:T(8,128)(2,1)} %copy.33) | copy-start | bytes 3145732
  118.9 3.2 %copy-start.10 = (f32[512]{0:T(512)S(1)}, f32[512]{0:T(512)}, u32[]{:S(2)}) copy-start(f32[512]{0:T(512)} %param.14) | copy-start | bytes 6148
  126.5 16.9 %collective-permute-start.4 = (bf16[1,512,1,1024]{1,3,2,0:T(8,128)(2,1)S(1)}, bf16[1,512,1,1024]{1,3,2,0:T(8,128)(2,1)S(1)}, u32[]{:S(2)}, u32[]{:S(2)}) collective-permute-start(bf16[1,512,1,1024]{1,3,2,0:T(8,128)(2,1)S(1)} %get-tuple-element.6), channel_id=1, source_target_pairs={{8,0},{16,8},{24,16},{9,1},{17,9},{25,17},{10,2},{18,10},{26,18},{... | collective-permute-start | bytes 3145736 | tf_op jit(solution)/shard_map/ppermute | solution.py:15
  128.4 16.1 %collective-permute-start.3 = (bf16[1,512,1,1024]{1,3,2,0:T(8,128)(2,1)S(1)}, bf16[1,512,1,1024]{1,3,2,0:T(8,128)(2,1)S(1)}, u32[]{:S(2)}, u32[]{:S(2)}) collective-permute-start(bf16[1,512,1,1024]{1,3,2,0:T(8,128)(2,1)S(1)} %get-tuple-element.6), channel_id=1, source_target_pairs={{0,8},{8,16},{16,24},{1,9},{9,17},{17,25},{2,10},{10,18},{18,26},{... | collective-permute-start | bytes 3145736 | tf_op jit(solution)/shard_map/ppermute | solution.py:15
  135.5 9.0 %copy-start.7 = (bf16[512,512]{1,0:T(8,128)(2,1)S(1)}, bf16[512,512]{1,0:T(8,128)(2,1)}, u32[]{:S(2)}) copy-start(bf16[512,512]{1,0:T(8,128)(2,1)} %param.10) | copy-start | bytes 1572868
  146.2 3.9 %copy-start.4 = (bf16[1,512,1,1024]{1,3,2,0:T(8,128)(2,1)}, bf16[1,512,1,1024]{1,3,2,0:T(8,128)(2,1)S(1)}, u32[]{:S(2)}) copy-start(bf16[1,512,1,1024]{1,3,2,0:T(8,128)(2,1)S(1)} %fusion.15) | copy-start | bytes 3145732
  160.4 44.3 %all-to-all-start.3 = ((bf16[8,2,32768]{2,1,0:T(2,128)(2,1)}), bf16[8,2,32768]{2,1,0:T(2,128)(2,1)S(1)}, u32[]{:S(2)}, u32[]{:S(2)}) async-start(bf16[8,2,32768]{2,1,0:T(2,128)(2,1)} %reshape.316), calls=%async_computation.3 | async-start | bytes 2097152 | tf_op jit(solution)/shard_map/all_to_all | solution.py:109
  166.1 17.3 %collective-permute-start.6 = (bf16[1,512,1,1024]{1,3,2,0:T(8,128)(2,1)}, bf16[1,512,1,1024]{1,3,2,0:T(8,128)(2,1)S(1)}, u32[]{:S(2)}, u32[]{:S(2)}) collective-permute-start(bf16[1,512,1,1024]{1,3,2,0:T(8,128)(2,1)} %copy-done.4), channel_id=1, source_target_pairs={{8,0},{16,8},{24,16},{9,1},{17,9},{25,17},{10,2},{18,10},{26,18},{... | collective-permute-start | bytes 3145736 | tf_op jit(solution)/shard_map/ppermute | solution.py:15
  168.0 16.7 %collective-permute-start.5 = (bf16[1,512,1,1024]{1,3,2,0:T(8,128)(2,1)}, bf16[1,512,1,1024]{1,3,2,0:T(8,128)(2,1)S(1)}, u32[]{:S(2)}, u32[]{:S(2)}) collective-permute-start(bf16[1,512,1,1024]{1,3,2,0:T(8,128)(2,1)} %copy-done.4), channel_id=1, source_target_pairs={{0,8},{8,16},{16,24},{1,9},{9,17},{17,25},{2,10},{10,18},{18,26},{... | collective-permute-start | bytes 3145736 | tf_op jit(solution)/shard_map/ppermute | solution.py:15
  175.8 9.0 %copy-start.5 = (bf16[1,512,1,1024]{1,3,2,0:T(8,128)(2,1)S(1)}, bf16[1,512,1,1024]{1,3,2,0:T(8,128)(2,1)}, u32[]{:S(2)}) copy-start(bf16[1,512,1,1024]{1,3,2,0:T(8,128)(2,1)} %copy-done.4) | copy-start | bytes 3145732
  175.8 9.0 %copy-start.8 = (bf16[512,512]{1,0:T(8,128)(2,1)S(1)}, bf16[512,512]{1,0:T(8,128)(2,1)}, u32[]{:S(2)}) copy-start(bf16[512,512]{1,0:T(8,128)(2,1)} %param.10) | copy-start | bytes 1572868
  175.8 9.0 %copy-start.13 = (f32[1,512,1,1024]{1,3,2,0:T(8,128)S(1)}, f32[1,512,1,1024]{1,3,2,0:T(8,128)}, u32[]{:S(2)}) copy-start(f32[1,512,1,1024]{1,3,2,0:T(8,128)} %get-tuple-element.7) | copy-start | bytes 6291460
  204.7 23.6 %all-to-all-start.4 = ((bf16[8,2,32768]{2,1,0:T(2,128)(2,1)}), bf16[8,2,32768]{2,1,0:T(2,128)(2,1)}, u32[]{:S(2)}, u32[]{:S(2)}) async-start(bf16[8,2,32768]{2,1,0:T(2,128)(2,1)} %reshape.318), calls=%async_computation.4 | async-start | bytes 2097152 | tf_op jit(solution)/shard_map/all_to_all | solution.py:109

commit v2 on v1

--- a/solution.py
+++ b/solution.py
@@ -1,6 +1,10 @@
+import functools
+
 import jax
 import jax.numpy as jnp
 from jax import lax
+from jax.experimental import pallas as pl
+from jax.experimental.pallas import tpu as pltpu
 from jax.sharding import PartitionSpec as P
 
 STEPS = 3
@@ -112,7 +116,518 @@
     return gather(history[-2]), gather(history[-1])
 
 
+MESH = pl.DeviceIdType.MESH
+POT, NEW, OLD, DAMP, OUT3, OUT4 = range(6)
+
+
+def packet_kernel(
+    n, hels,
+    newer, older, kinetic, transform, potential, coupling, weight, damping,
+    out_old, out_new,
+    newer_v, older_v, kin, tr, pot_in, pot_wide, coef, coef_low, damp_own, damp_all, weight_all,
+    damp_col, weight_col, send_pot, send_new, send_old, pot, x0, x1, x2, x3, x4, total, grid,
+    low, high, back3, back4,
+    in_sem, lane_sem, out_sem, rad_send, rad_recv, pot_send, pot_recv, hel_send, hel_recv, coef_sem,
+):
+    me = lax.axis_index("rad")
+    hel = lax.axis_index("hel")
+    rows = send_new.shape[1]
+    ang = newer.shape[1]
+    width = ang // hels
+    has_low = hel > 0
+    has_high = hel < hels - 1
+
+    def shift(i):
+        if n % 2:
+            return i + 1
+        return n // 2 + ((i + 1) // 2) * (1 - 2 * (i % 2))
+
+    def target(i):
+        return lax.rem(me + shift(i), n)
+
+    def source(i):
+        return lax.rem(me - shift(i) + n, n)
+
+    def block(c):
+        return pl.ds(pl.multiple_of(c * rows, rows), rows)
+
+    loads = [
+        pltpu.make_async_copy(src, dst, in_sem.at[s])
+        for s, (src, dst) in enumerate(
+            (
+                (potential.at[:, :, pl.ds(pl.multiple_of(hel * width, width), width)], pot_in),
+                (damping, damp_own),
+                (coupling, coef),
+                (weight, weight_all),
+                (kinetic, kin),
+                (transform, tr),
+            )
+        )
+    ]
+
+    def lanes(l):
+        return pl.ds(pl.multiple_of(l * 128, 128), 128)
+
+    def newer_load(l):
+        return pltpu.make_async_copy(newer.at[:, lanes(l)], newer_v.at[l], lane_sem.at[0, l])
+
+    def older_load(l):
+        return pltpu.make_async_copy(older.at[:, lanes(l)], older_v.at[l], lane_sem.at[1, l])
+
+    def each_lane(copy, method):
+        @pl.loop(0, ang // 128)
+        def _(l):
+            getattr(copy(l), method)()
+
+    for load in loads[:3]:
+        load.start()
+    each_lane(newer_load, "start")
+    each_lane(older_load, "start")
+    for load in loads[3:]:
+        load.start()
+
+    barrier = pltpu.get_barrier_semaphore()
+
+    @pl.loop(1, n)
+    def _(j):
+        pl.semaphore_signal(
+            barrier, inc=1, device_id={"rad": lax.rem(me + j, n)}, device_id_type=MESH
+        )
+
+    @pl.loop(1, hels)
+    def _(j):
+        pl.semaphore_signal(
+            barrier, inc=1, device_id={"hel": lax.rem(hel + j, hels)}, device_id_type=MESH
+        )
+
+    pl.semaphore_wait(barrier, n + hels - 2)
+
+    def over_rad(kind, src, dst, i):
+        return pltpu.make_async_remote_copy(
+            src_ref=src,
+            dst_ref=dst,
+            send_sem=rad_send.at[kind, i],
+            recv_sem=rad_recv.at[kind, i],
+            device_id={"rad": target(i)},
+            device_id_type=MESH,
+        )
+
+    def pot_copy(i):
+        return over_rad(POT, send_pot.at[i], pot.at[hel, block(me)], i)
+
+    def new_copy(i):
+        return over_rad(NEW, send_new.at[i], x1.at[block(me)], i)
+
+    def old_copy(i):
+        return over_rad(OLD, send_old.at[i], x0.at[block(me)], i)
+
+    def damp_copy(i):
+        return over_rad(DAMP, damp_own, damp_all.at[me], i)
+
+    def out3_copy(i):
+        return over_rad(OUT3, x3.at[block(target(i))], back3.at[me], i)
+
+    def out4_copy(i):
+        return over_rad(OUT4, x4.at[block(target(i))], back4.at[me], i)
+
+    def pot_share(j):
+        return pltpu.make_async_remote_copy(
+            src_ref=pot.at[hel],
+            dst_ref=pot.at[hel],
+            send_sem=pot_send.at[j],
+            recv_sem=pot_recv.at[j],
+            device_id={"hel": lax.rem(hel + j, hels)},
+            device_id_type=MESH,
+        )
+
+    coef_copy = pltpu.make_async_remote_copy(
+        src_ref=coef,
+        dst_ref=coef_low,
+        send_sem=coef_sem.at[0],
+        recv_sem=coef_sem.at[1],
+        device_id={"hel": lax.rem(hel + 1, hels)},
+        device_id_type=MESH,
+    )
+
+    def hel_up(step, x, c, sem):
+        return pltpu.make_async_remote_copy(
+            src_ref=x.at[c],
+            dst_ref=low.at[step, c],
+            send_sem=hel_send.at[step, 0, sem],
+            recv_sem=hel_recv.at[step, 0, sem],
+            device_id={"hel": lax.rem(hel + 1, hels)},
+            device_id_type=MESH,
+        )
+
+    def hel_down(step, x, c, sem):
+        return pltpu.make_async_remote_copy(
+            src_ref=x.at[c],
+            dst_ref=high.at[step, c],
+            send_sem=hel_send.at[step, 1, sem],
+            recv_sem=hel_recv.at[step, 1, sem],
+            device_id={"hel": lax.rem(hel - 1 + hels, hels)},
+            device_id_type=MESH,
+        )
+
+    def hel_start(step, x, c, sem):
+        @pl.when(has_high)
+        def _():
+            hel_up(step, x, c, sem).start()
+
+        @pl.when(has_low)
+        def _():
+            hel_down(step, x, c, sem).start()
+
+    def hel_wait_recv(step, x, c, sem):
+        @pl.when(has_low)
+        def _():
+            hel_up(step, x, c, sem).wait_recv()
+
+        @pl.when(has_high)
+        def _():
+            hel_down(step, x, c, sem).wait_recv()
+
+    def hel_wait_send(step, x, c, sem):
+        @pl.when(has_high)
+        def _():
+            hel_up(step, x, c, sem).wait_send()
+
+        @pl.when(has_low)
+        def _():
+            hel_down(step, x, c, sem).wait_send()
+
+    def trailing(make, copy):
+        @pl.loop(0, n - 1)
+        def _(i):
+            make(i)
+
+            @pl.when(i > 0)
+            def _():
+                copy(i - 1).start()
+
+    everything = pl.ds(0, n * rows)
+
+    loads[0].wait()
+    for l in range(width // 128):
+        part = pot_in[:, :, 128 * l : 128 * (l + 1)].astype(jnp.float32)
+        pot_wide[l] = part.reshape(pot_wide.shape[1:])
+
+    def picked(ref, c):
+        return jnp.concatenate(
+            [
+                ref[l, pl.ds(c, rows, stride=n), :]
+                for l in range(ref.shape[0])
+            ],
+            axis=1,
+        ).astype(jnp.bfloat16)
+
+    def make_pot(i):
+        send_pot[i] = picked(pot_wide, target(i))
+
+    trailing(make_pot, pot_copy)
+    pot[hel, block(me)] = picked(pot_wide, me)
+    pot_copy(n - 2).start()
+
+    each_lane(newer_load, "wait")
+
+    def make_new(i):
+        send_new[i] = picked(newer_v, target(i))
+
+    trailing(make_new, new_copy)
+    x1[block(me)] = picked(newer_v, me)
+    new_copy(n - 2).start()
+
+    loads[1].wait()
+    loads[2].wait()
+
+    @pl.loop(0, n - 1)
+    def _(i):
+        damp_copy(i).start()
+
+    @pl.when(has_high)
+    def _():
+        coef_copy.start()
+
+    each_lane(older_load, "wait")
+
+    def make_old(i):
+        send_old[i] = picked(older_v, target(i))
+
+    trailing(make_old, old_copy)
+    x0[block(me)] = picked(older_v, me)
+    old_copy(n - 2).start()
+    damp_all[me] = damp_own[...]
+
+    @pl.when(jnp.logical_not(has_low))
+    def _():
+        low[...] = jnp.zeros_like(low)
+        coef_low[...] = jnp.zeros_like(coef_low)
+
+    @pl.when(jnp.logical_not(has_high))
+    def _():
+        high[...] = jnp.zeros_like(high)
+
+    for load in loads[3:]:
+        load.wait()
+
+    @pl.loop(0, n - 1)
+    def _(i):
+        pot_copy(i).wait_recv()
+
+    @pl.loop(1, hels)
+    def _(j):
+        pot_share(j).start()
+
+    @pl.loop(0, n - 1)
+    def _(i):
+        damp_copy(i).wait_recv()
+
+    @pl.when(has_low)
+    def _():
+        coef_copy.wait_recv()
+
+    line = lax.broadcasted_iota(jnp.int32, (rows, rows), 0)
+    lane = lax.broadcasted_iota(jnp.int32, (rows, rows), 1)
+
+    def column(row):
+        diagonal = jnp.where(line == lane, jnp.broadcast_to(row, (rows, rows)), 0.0)
+        return jnp.broadcast_to(jnp.sum(diagonal, axis=1, keepdims=True), (rows, 128))
+
+    @pl.loop(0, n)
+    def _(c):
+        damp_col[block(c)] = column(damp_all[c])
+        weight_col[block(c)] = column(weight_all[c])
+
+    @pl.loop(0, n - 1)
+    def _(i):
+        new_copy(i).wait_recv()
+
+    hel_start(0, x1, everything, 0)
+
+    @pl.loop(1, hels)
+    def _(j):
+        pot_share(j).wait_recv()
+
+    def tile(t):
+        return pl.ds(pl.multiple_of(t * width, width), width)
+
+    def multiply(x):
+        @pl.loop(0, hels)
+        def _(t):
+            values = jnp.dot(x[...], tr[:, tile(t)], preferred_element_type=jnp.float32)
+            grid[:, tile(t)] = (values * pot[t].astype(jnp.float32)).astype(jnp.bfloat16)
+
+        @pl.loop(0, hels)
+        def _(t):
+            radial = jnp.dot(kin[...], x[:, tile(t)], preferred_element_type=jnp.float32)
+            angular = lax.dot_general(
+                grid[...],
+                tr[tile(t), :],
+                (((1,), (1,)), ((), ())),
+                preferred_element_type=jnp.float32,
+            )
+            total[:, tile(t)] = radial + angular
+
+    lower_coef = coef_low[...].astype(jnp.float32)
+    upper_coef = coef[...].astype(jnp.float32)
+
+    def finish(step, prev, c):
+        span = block(c)
+        damp = damp_col[span, 0:1]
+        mixed = lower_coef * low[step, span].astype(jnp.float32)
+        mixed = mixed + upper_coef * high[step, span].astype(jnp.float32)
+        applied = SCALE_FACTOR * (total[span] + weight_col[span, 0:1] * mixed)
+        following = damp * (2.0 * applied - damp * prev[span].astype(jnp.float32))
+        return following.astype(jnp.bfloat16)
+
+    multiply(x1)
+    hel_wait_recv(0, x1, everything, 0)
+    x2[block(me)] = finish(0, x0, me)
+
+    @pl.loop(0, n - 1)
+    def _(i):
+        old_copy(i).wait_recv()
+        x2[block(source(i))] = finish(0, x0, source(i))
+
+        @pl.when(i == 0)
+        def _():
+            hel_start(1, x2, block(me), 0)
+
+        @pl.when(i > 0)
+        def _():
+            hel_start(1, x2, block(source(i - 1)), n - shift(i - 1))
+
+    hel_start(1, x2, block(source(n - 2)), n - shift(n - 2))
+
+    multiply(x2)
+
+    @pl.loop(0, n)
+    def _(i):
+        hel_wait_recv(1, x2, block(lax.rem(me + i, n)), i)
+
+    def make_out3(i):
+        x3[block(target(i))] = finish(1, x1, target(i))
+
+    trailing(make_out3, out3_copy)
+    mine = finish(1, x1, me)
+    x3[block(me)] = mine
+    back3[me] = mine
+    out3_copy(n - 2).start()
+    hel_start(2, x3, everything, 0)
+
+    multiply(x3)
+    hel_wait_recv(2, x3, everything, 0)
+
+    def make_out4(i):
+        x4[block(target(i))] = finish(2, x2, target(i))
+
+    trailing(make_out4, out4_copy)
+    mine = finish(2, x2, me)
+    x4[block(me)] = mine
+    back4[me] = mine
+    out4_copy(n - 2).start()
+
+    def placed(ref, c, values):
+        for l in range(ang // 128):
+            ref[l, pl.ds(c, rows, stride=n), :] = values[
+                :, 128 * l : 128 * (l + 1)
+            ].astype(jnp.float32)
+
+    def unload(wide, out, s, l):
+        return pltpu.make_async_copy(wide.at[l], out.at[:, lanes(l)], out_sem.at[s, l])
+
+    for copy, back, wide, out, s in (
+        (out3_copy, back3, newer_v, out_old, 0),
+        (out4_copy, back4, older_v, out_new, 1),
+    ):
+        placed(wide, me, back[me])
+
+        @pl.loop(0, n - 1)
+        def _(i):
+            copy(i).wait_recv()
+            placed(wide, source(i), back[source(i)])
+
+        each_lane(functools.partial(unload, wide, out, s), "start")
+
+    @pl.loop(0, n - 1)
+    def _(i):
+        for copy in (pot_copy, new_copy, old_copy, damp_copy, out3_copy, out4_copy):
+            copy(i).wait_send()
+
+    @pl.loop(1, hels)
+    def _(j):
+        pot_share(j).wait_send()
+
+    @pl.when(has_high)
+    def _():
+        coef_copy.wait_send()
+
+    hel_wait_send(0, x1, everything, 0)
+    hel_wait_send(2, x3, everything, 0)
+
+    @pl.loop(0, n)
+    def _(i):
+        hel_wait_send(1, x2, block(lax.rem(me + i, n)), i)
+
+    each_lane(functools.partial(unload, newer_v, out_old, 0), "wait")
+    each_lane(functools.partial(unload, older_v, out_new, 1), "wait")
+
+
+def one_vibration(
+    older_packet, newer_packet, kinetic, transform, potential, coupling, radial_weight, damping
+):
+    _, rows, n, ang = newer_packet.shape
+    hels = lax.axis_size("hel")
+    width = ang // hels
+    points = n * rows
+    bf16, f32 = jnp.bfloat16, jnp.float32
+    vector = pltpu.VMEM((points, ang), bf16)
+    blocks = pltpu.VMEM((n, rows, ang), bf16)
+    wide = pltpu.VMEM((points, ang), f32)
+    flat = jax.ShapeDtypeStruct((points, ang), f32)
+    anywhere = pl.BlockSpec(memory_space=pl.ANY)
+    sem = pltpu.SemaphoreType.DMA
+    outs = pl.pallas_call(
+        functools.partial(packet_kernel, n, hels),
+        out_shape=(flat, flat),
+        in_specs=[anywhere] * 8,
+        out_specs=(anywhere, anywhere),
+        scratch_shapes=[
+            pltpu.VMEM((ang // 128, points, 128), f32),
+            pltpu.VMEM((ang // 128, points, 128), f32),
+            pltpu.VMEM((points, points), bf16),
+            pltpu.VMEM((ang, ang), bf16),
+            pltpu.VMEM((rows, n, width), bf16),
+            pltpu.VMEM((width // 128, points, 128), f32),
+            pltpu.VMEM((1, ang), bf16),
+            pltpu.VMEM((1, ang), bf16),
+            pltpu.VMEM((1, rows), f32),
+            pltpu.VMEM((n, 1, rows), f32),
+            pltpu.VMEM((n, 1, rows), f32),
+            pltpu.VMEM((points, 128), f32),
+            pltpu.VMEM((points, 128), f32),
+            pltpu.VMEM((n, rows, width), bf16),
+            blocks,
+            blocks,
+            pltpu.VMEM((hels, points, width), bf16),
+            vector,
+            vector,
+            vector,
+            vector,
+            vector,
+            wide,
+            vector,
+            pltpu.VMEM((STEPS, points, ang), bf16),
+            pltpu.VMEM((STEPS, points, ang), bf16),
+            blocks,
+            blocks,
+            sem((6,)),
+            sem((2, ang // 128)),
+            sem((2, ang // 128)),
+            sem((6, n)),
+            sem((6, n)),
+            sem((hels,)),
+            sem((hels,)),
+            sem((STEPS, 2, n)),
+            sem((STEPS, 2, n)),
+            sem((2,)),
+        ],
+        compiler_params=pltpu.CompilerParams(
+            collective_id=0, has_side_effects=True, vmem_limit_bytes=60 * 1024 * 1024
+        ),
+    )(
+        newer_packet.reshape(points, ang),
+        older_packet.reshape(points, ang),
+        kinetic,
+        transform[0],
+        potential,
+        coupling,
+        radial_weight.reshape(n, 1, rows),
+        damping.reshape(1, rows),
+    )
+    shape = newer_packet.shape
+    return outs[0].reshape(shape), outs[1].reshape(shape)
+
+
+def fits(packet):
+    hel_rows, rows, vibs, ang = packet.shape
+    hels = lax.axis_size("hel")
+    return (
+        STEPS == 3
+        and hel_rows == 1
+        and vibs == lax.axis_size("rad")
+        and vibs > 1
+        and hels > 1
+        and rows % 16 == 0
+        and ang % (hels * 128) == 0
+        and rows * vibs <= 512
+        and ang <= 1024
+    )
+
+
 def whole_body(older_packet, newer_packet, *rest):
+    if fits(newer_packet):
+        return one_vibration(older_packet, newer_packet, *rest)
     if newer_packet.shape[2] % lax.axis_size("rad") == 0:
         return by_vibration(older_packet, newer_packet, *rest)
     return body(older_packet, newer_packet, *rest)

time: 240 us -> 121 us (0.50)
  the two profiles are of different devices: /device:TPU:1 before, /device:TPU:11 now
where the time goes in v2:
time: 121 us
  Pallas kernels  114 us (94%)
  local copies, waits for them, and re-layouts  5.99 us (5%)
    pallas_call x1, Pallas kernels, one_vibration(): pl.pallas_call(functools.partial(packet_kernel, n, hels), out_shape=(flat...  114 us
    unnamed x4, local copies, waits for them, and re-layouts  4.63 us

profile of v2, /device:TPU:11, one launch (start us, length us, event | category | flops | bytes accessed | tf_op | source)
XLA Modules:
  0.0 121.0 jit_solution(6221102775814785339)
XLA Ops:
  0.6 1.4 %reshape.24.weight = f32[8,1,64]{2,1,0:T(1,128)} reshape(f32[512]{0:T(512)} %param.14) | data formatting | bytes 4096 | tf_op jit(solution)/shard_map/reshape | solution.py:605
  2.0 114.4 %shard_map.95 = (f32[512,1024]{1,0:T(8,128)}, f32[512,1024]{1,0:T(8,128)}) custom-call(f32[512,1024]{1,0:T(8,128)} %bitcast.6, f32[512,1024]{1,0:T(8,128)} %bitcast.7, bf16[512,512]{1,0:T(8,128)(2,1)} %kinetic.1, bf16[1024,1024]{1,0:T(8,128)(2,1)} %bitcast.8, bf16[64,8,1024]{2,1,0:T(8,128)(2,1)} %potential.1, bf16[1,1024]{1,0:T(2,128)(2,1)} %coupling.1, ...), custom_call_target="tpu_custom_call" | custom-call | tf_op jit(solution)/shard_map/pallas_call | solution.py:550
  116.4 0.0 copy-start
  116.4 3.3 %copy.12 = f32[1,64,8,1024]{3,2,1,0:T(8,128)} copy(f32[1,64,8,1024]{3,2,1,0:T(8,128)} %bitcast.10) | data formatting | bytes 4194304
  119.7 0.0 copy-done
  119.7 1.3 %copy.13 = f32[1,64,8,1024]{3,2,1,0:T(8,128)} copy(f32[1,64,8,1024]{3,2,1,0:T(8,128)S(1)} %bitcast.9) | data formatting | bytes 4194304
Async XLA Ops:
  116.4 3.3 %copy-start = (f32[512,1024]{1,0:T(8,128)S(1)}, f32[512,1024]{1,0:T(8,128)}, u32[]{:S(2)}) copy-start(f32[512,1024]{1,0:T(8,128)} %get-tuple-element.5) | copy-start | bytes 6291460

commit v3 on v2

--- a/solution.py
+++ b/solution.py
@@ -123,11 +123,11 @@
 def packet_kernel(
     n, hels,
     newer, older, kinetic, transform, potential, coupling, weight, damping,
-    out_old, out_new,
+    back3, back4,
     newer_v, older_v, kin, tr, pot_in, pot_wide, coef, coef_low, damp_own, damp_all, weight_all,
     damp_col, weight_col, send_pot, send_new, send_old, pot, x0, x1, x2, x3, x4, total, grid,
-    low, high, back3, back4,
-    in_sem, lane_sem, out_sem, rad_send, rad_recv, pot_send, pot_recv, hel_send, hel_recv, coef_sem,
+    low, high,
+    in_sem, lane_sem, own_sem, rad_send, rad_recv, pot_send, pot_recv, hel_send, hel_recv, coef_sem,
 ):
     me = lax.axis_index("rad")
     hel = lax.axis_index("hel")
@@ -396,13 +396,17 @@
     @pl.loop(0, n)
     def _(c):
         damp_col[block(c)] = column(damp_all[c])
-        weight_col[block(c)] = column(weight_all[c])
+
+    for c in range(n):
+        part = weight_all[:, c * rows : (c + 1) * rows]
+        weight_col[c * rows : (c + 1) * rows] = column(part)
+
+    hel_start(0, x1, block(me), 0)
 
     @pl.loop(0, n - 1)
     def _(i):
         new_copy(i).wait_recv()
-
-    hel_start(0, x1, everything, 0)
+        hel_start(0, x1, block(source(i)), n - shift(i))
 
     @pl.loop(1, hels)
     def _(j):
@@ -410,6 +414,24 @@
 
     def tile(t):
         return pl.ds(pl.multiple_of(t * width, width), width)
+
+    def angular_block(x, span, between):
+        @pl.loop(0, hels)
+        def _(t):
+            values = jnp.dot(x[span], tr[:, tile(t)], preferred_element_type=jnp.float32)
+            values = values * pot[t, span].astype(jnp.float32)
+            grid[span, tile(t)] = values.astype(jnp.bfloat16)
+
+        between()
+
+        @pl.loop(0, hels)
+        def _(t):
+            total[span, tile(t)] = lax.dot_general(
+                grid[span],
+                tr[tile(t), :],
+                (((1,), (1,)), ((), ())),
+                preferred_element_type=jnp.float32,
+            )
 
     def multiply(x):
         @pl.loop(0, hels)
@@ -441,37 +463,38 @@
         return following.astype(jnp.bfloat16)
 
     multiply(x1)
-    hel_wait_recv(0, x1, everything, 0)
-    x2[block(me)] = finish(0, x0, me)
+
+    def hel_arrived(step, x):
+        @pl.loop(0, n)
+        def _(i):
+            hel_wait_recv(step, x, block(lax.rem(me + i, n)), i)
+
+    hel_arrived(0, x1)
+
+    def next_block(c, sem):
+        x2[block(c)] = finish(0, x0, c)
+        angular_block(x2, block(c), lambda: hel_start(1, x2, block(c), sem))
+
+    next_block(me, 0)
 
     @pl.loop(0, n - 1)
     def _(i):
         old_copy(i).wait_recv()
-        x2[block(source(i))] = finish(0, x0, source(i))
-
-        @pl.when(i == 0)
-        def _():
-            hel_start(1, x2, block(me), 0)
-
-        @pl.when(i > 0)
-        def _():
-            hel_start(1, x2, block(source(i - 1)), n - shift(i - 1))
-
-    hel_start(1, x2, block(source(n - 2)), n - shift(n - 2))
-
-    multiply(x2)
-
-    @pl.loop(0, n)
-    def _(i):
-        hel_wait_recv(1, x2, block(lax.rem(me + i, n)), i)
+        next_block(source(i), n - shift(i))
+
+    @pl.loop(0, hels)
+    def _(t):
+        total[:, tile(t)] += jnp.dot(
+            kin[...], x2[:, tile(t)], preferred_element_type=jnp.float32
+        )
+
+    hel_arrived(1, x2)
 
     def make_out3(i):
         x3[block(target(i))] = finish(1, x1, target(i))
 
     trailing(make_out3, out3_copy)
-    mine = finish(1, x1, me)
-    x3[block(me)] = mine
-    back3[me] = mine
+    x3[block(me)] = finish(1, x1, me)
     out3_copy(n - 2).start()
     hel_start(2, x3, everything, 0)
 
@@ -482,32 +505,20 @@
         x4[block(target(i))] = finish(2, x2, target(i))
 
     trailing(make_out4, out4_copy)
-    mine = finish(2, x2, me)
-    x4[block(me)] = mine
-    back4[me] = mine
+    x4[block(me)] = finish(2, x2, me)
     out4_copy(n - 2).start()
 
-    def placed(ref, c, values):
-        for l in range(ang // 128):
-            ref[l, pl.ds(c, rows, stride=n), :] = values[
-                :, 128 * l : 128 * (l + 1)
-            ].astype(jnp.float32)
-
-    def unload(wide, out, s, l):
-        return pltpu.make_async_copy(wide.at[l], out.at[:, lanes(l)], out_sem.at[s, l])
-
-    for copy, back, wide, out, s in (
-        (out3_copy, back3, newer_v, out_old, 0),
-        (out4_copy, back4, older_v, out_new, 1),
-    ):
-        placed(wide, me, back[me])
-
-        @pl.loop(0, n - 1)
-        def _(i):
-            copy(i).wait_recv()
-            placed(wide, source(i), back[source(i)])
-
-        each_lane(functools.partial(unload, wide, out, s), "start")
+    own = [
+        pltpu.make_async_copy(x.at[block(me)], back.at[me], own_sem.at[j])
+        for j, (x, back) in enumerate(((x3, back3), (x4, back4)))
+    ]
+    for copy in own:
+        copy.start()
+
+    @pl.loop(0, n - 1)
+    def _(i):
+        out3_copy(i).wait_recv()
+        out4_copy(i).wait_recv()
 
     @pl.loop(0, n - 1)
     def _(i):
@@ -522,15 +533,42 @@
     def _():
         coef_copy.wait_send()
 
-    hel_wait_send(0, x1, everything, 0)
     hel_wait_send(2, x3, everything, 0)
 
     @pl.loop(0, n)
     def _(i):
+        hel_wait_send(0, x1, block(lax.rem(me + i, n)), i)
         hel_wait_send(1, x2, block(lax.rem(me + i, n)), i)
 
-    each_lane(functools.partial(unload, newer_v, out_old, 0), "wait")
-    each_lane(functools.partial(unload, older_v, out_new, 1), "wait")
+    for copy in own:
+        copy.wait()
+
+
+def place_kernel(n, back3, back4, out_old, out_new, held, wide, in_sem, out_sem):
+    rows, ang = back3.shape[1:]
+    groups = ang // 128
+    pairs = ((back3, out_old), (back4, out_new))
+
+    def load(s, l):
+        return pltpu.make_async_copy(
+            pairs[s][0].at[:, :, pl.ds(128 * l, 128)], held.at[s, l], in_sem.at[s, l]
+        )
+
+    def unload(s, l):
+        return pltpu.make_async_copy(
+            wide.at[s, l], pairs[s][1].at[:, pl.ds(128 * l, 128)], out_sem.at[s, l]
+        )
+
+    every = [(s, l) for s in range(2) for l in range(groups)]
+    for s, l in every:
+        load(s, l).start()
+    for s, l in every:
+        load(s, l).wait()
+        for c in range(n):
+            wide[s, l, pl.ds(c, rows, stride=n), :] = held[s, l, c].astype(jnp.float32)
+        unload(s, l).start()
+    for s, l in every:
+        unload(s, l).wait()
 
 
 def one_vibration(
@@ -545,11 +583,13 @@
     blocks = pltpu.VMEM((n, rows, ang), bf16)
     wide = pltpu.VMEM((points, ang), f32)
     flat = jax.ShapeDtypeStruct((points, ang), f32)
+    back = jax.ShapeDtypeStruct((n, rows, ang), bf16)
     anywhere = pl.BlockSpec(memory_space=pl.ANY)
     sem = pltpu.SemaphoreType.DMA
-    outs = pl.pallas_call(
+    groups = ang // 128
+    backs = pl.pallas_call(
         functools.partial(packet_kernel, n, hels),
-        out_shape=(flat, flat),
+        out_shape=(back, back),
         in_specs=[anywhere] * 8,
         out_specs=(anywhere, anywhere),
         scratch_shapes=[
@@ -563,7 +603,7 @@
             pltpu.VMEM((1, ang), bf16),
             pltpu.VMEM((1, rows), f32),
             pltpu.VMEM((n, 1, rows), f32),
-            pltpu.VMEM((n, 1, rows), f32),
+            pltpu.VMEM((1, points), f32),
             pltpu.VMEM((points, 128), f32),
             pltpu.VMEM((points, 128), f32),
             pltpu.VMEM((n, rows, width), bf16),
@@ -579,11 +619,9 @@
             vector,
             pltpu.VMEM((STEPS, points, ang), bf16),
             pltpu.VMEM((STEPS, points, ang), bf16),
-            blocks,
-            blocks,
             sem((6,)),
-            sem((2, ang // 128)),
-            sem((2, ang // 128)),
+            sem((2, groups)),
+            sem((2,)),
             sem((6, n)),
             sem((6, n)),
             sem((hels,)),
@@ -602,9 +640,21 @@
         transform[0],
         potential,
         coupling,
-        radial_weight.reshape(n, 1, rows),
+        radial_weight.reshape(1, points),
         damping.reshape(1, rows),
     )
+    outs = pl.pallas_call(
+        functools.partial(place_kernel, n),
+        out_shape=(flat, flat),
+        in_specs=[anywhere] * 2,
+        out_specs=(anywhere, anywhere),
+        scratch_shapes=[
+            pltpu.VMEM((2, groups, n, rows, 128), bf16),
+            pltpu.VMEM((2, groups, points, 128), f32),
+            sem((2, groups)),
+            sem((2, groups)),
+        ],
+    )(*backs)
     shape = newer_packet.shape
     return outs[0].reshape(shape), outs[1].reshape(shape)
 

time: 121 us -> 132 us (1.091)
  Pallas kernels: 114 us -> 131 us
  local copies, waits for them, and re-layouts: 5.99 us -> 0 us
    pallas_call x1 -> x2, Pallas kernels: 114 us -> 131 us  [the longest x1 128 us: one_vibration(): pl.pallas_call(functools.partial(packet_kernel, n, hels), out_shape=(back...]
    unnamed x4 -> x0, local copies, waits for them, and re-layouts: 4.63 us -> none
    reshape x1 -> x0, local copies, waits for them, and re-layouts: 1.36 us -> none  [one_vibration(): radial_weight.reshape(n, 1, rows)]
where the time goes in v3:
time: 132 us
  Pallas kernels  131 us (99%)
    pallas_call x1, Pallas kernels, one_vibration(): pl.pallas_call(functools.partial(packet_kernel, n, hels), out_shape=(back...  128 us
    pallas_call x1, Pallas kernels, one_vibration(): pl.pallas_call(functools.partial(place_kernel, n), out_shape=(flat, flat)...  3.24 us

profile of v3, /device:TPU:11, one launch (start us, length us, event | category | flops | bytes accessed | tf_op | source)
XLA Modules:
  0.0 131.9 jit_solution(5731123541771641820)
XLA Ops:
  0.6 128.1 %shard_map.95 = (bf16[8,64,1024]{2,1,0:T(8,128)(2,1)}, bf16[8,64,1024]{2,1,0:T(8,128)(2,1)}) custom-call(f32[512,1024]{1,0:T(8,128)} %bitcast.7, f32[512,1024]{1,0:T(8,128)} %bitcast.8, bf16[512,512]{1,0:T(8,128)(2,1)} %kinetic.1, bf16[1024,1024]{1,0:T(8,128)(2,1)} %bitcast.9, bf16[64,8,1024]{2,1,0:T(8,128)(2,1)} %potential.1, bf16[1,1024]{1,0:T(2,128)(2,1)} %coupling.1, ...), custom_call_target="tpu_custom_call" | custom-call | tf_op jit(solution)/shard_map/pallas_call | solution.py:590
  128.7 3.2 %shard_map.96 = (f32[512,1024]{1,0:T(8,128)}, f32[512,1024]{1,0:T(8,128)}) custom-call(bf16[8,64,1024]{2,1,0:T(8,128)(2,1)} %get-tuple-element.6.back3, bf16[8,64,1024]{2,1,0:T(8,128)(2,1)} %get-tuple-element.7.back4), custom_call_target="tpu_custom_call" | custom-call | tf_op jit(solution)/shard_map/pallas_call | solution.py:646

commit v4 on v3

--- a/solution.py
+++ b/solution.py
@@ -412,43 +412,23 @@
     def _(j):
         pot_share(j).wait_recv()
 
-    def tile(t):
-        return pl.ds(pl.multiple_of(t * width, width), width)
-
-    def angular_block(x, span, between):
-        @pl.loop(0, hels)
-        def _(t):
-            values = jnp.dot(x[span], tr[:, tile(t)], preferred_element_type=jnp.float32)
-            values = values * pot[t, span].astype(jnp.float32)
-            grid[span, tile(t)] = values.astype(jnp.bfloat16)
-
-        between()
-
-        @pl.loop(0, hels)
-        def _(t):
-            total[span, tile(t)] = lax.dot_general(
-                grid[span],
-                tr[tile(t), :],
-                (((1,), (1,)), ((), ())),
-                preferred_element_type=jnp.float32,
-            )
+    def to_grid(x, span):
+        values = jnp.dot(x[span], tr[...], preferred_element_type=jnp.float32)
+        for t in range(hels):
+            part = values[:, t * width : (t + 1) * width] * pot[t, span].astype(jnp.float32)
+            grid[span, t * width : (t + 1) * width] = part.astype(jnp.bfloat16)
+
+    def from_grid(span):
+        return lax.dot_general(
+            grid[span], tr[...], (((1,), (1,)), ((), ())), preferred_element_type=jnp.float32
+        )
+
+    def radial(x):
+        return jnp.dot(kin[...], x[...], preferred_element_type=jnp.float32)
 
     def multiply(x):
-        @pl.loop(0, hels)
-        def _(t):
-            values = jnp.dot(x[...], tr[:, tile(t)], preferred_element_type=jnp.float32)
-            grid[:, tile(t)] = (values * pot[t].astype(jnp.float32)).astype(jnp.bfloat16)
-
-        @pl.loop(0, hels)
-        def _(t):
-            radial = jnp.dot(kin[...], x[:, tile(t)], preferred_element_type=jnp.float32)
-            angular = lax.dot_general(
-                grid[...],
-                tr[tile(t), :],
-                (((1,), (1,)), ((), ())),
-                preferred_element_type=jnp.float32,
-            )
-            total[:, tile(t)] = radial + angular
+        to_grid(x, everything)
+        total[...] = from_grid(everything) + radial(x)
 
     lower_coef = coef_low[...].astype(jnp.float32)
     upper_coef = coef[...].astype(jnp.float32)
@@ -473,7 +453,9 @@
 
     def next_block(c, sem):
         x2[block(c)] = finish(0, x0, c)
-        angular_block(x2, block(c), lambda: hel_start(1, x2, block(c), sem))
+        to_grid(x2, block(c))
+        hel_start(1, x2, block(c), sem)
+        total[block(c)] = from_grid(block(c))
 
     next_block(me, 0)
 
@@ -482,12 +464,7 @@
         old_copy(i).wait_recv()
         next_block(source(i), n - shift(i))
 
-    @pl.loop(0, hels)
-    def _(t):
-        total[:, tile(t)] += jnp.dot(
-            kin[...], x2[:, tile(t)], preferred_element_type=jnp.float32
-        )
-
+    total[...] += radial(x2)
     hel_arrived(1, x2)
 
     def make_out3(i):

time: 132 us -> 126 us (0.955)
  Pallas kernels: 131 us -> 125 us
    pallas_call x1, Pallas kernels: 128 us -> 122 us  [one_vibration(): pl.pallas_call(functools.partial(packet_kernel, n, hels), out_shape=(back...]
where the time goes in v4:
time: 126 us
  Pallas kernels  125 us (99%)
    pallas_call x1, Pallas kernels, one_vibration(): pl.pallas_call(functools.partial(packet_kernel, n, hels), out_shape=(back...  122 us
    pallas_call x1, Pallas kernels, one_vibration(): pl.pallas_call(functools.partial(place_kernel, n), out_shape=(flat, flat)...  3.24 us

profile of v4, /device:TPU:11, one launch (start us, length us, event | category | flops | bytes accessed | tf_op | source)
XLA Modules:
  0.0 125.8 jit_solution(11696569339733689354)
XLA Ops:
  0.6 121.9 %shard_map.95 = (bf16[8,64,1024]{2,1,0:T(8,128)(2,1)}, bf16[8,64,1024]{2,1,0:T(8,128)(2,1)}) custom-call(f32[512,1024]{1,0:T(8,128)} %bitcast.7, f32[512,1024]{1,0:T(8,128)} %bitcast.8, bf16[512,512]{1,0:T(8,128)(2,1)} %kinetic.1, bf16[1024,1024]{1,0:T(8,128)(2,1)} %bitcast.9, bf16[64,8,1024]{2,1,0:T(8,128)(2,1)} %potential.1, bf16[1,1024]{1,0:T(2,128)(2,1)} %coupling.1, ...), custom_call_target="tpu_custom_call" | custom-call | tf_op jit(solution)/shard_map/pallas_call | solution.py:567
  122.5 3.2 %shard_map.96 = (f32[512,1024]{1,0:T(8,128)}, f32[512,1024]{1,0:T(8,128)}) custom-call(bf16[8,64,1024]{2,1,0:T(8,128)(2,1)} %get-tuple-element.6.back3, bf16[8,64,1024]{2,1,0:T(8,128)(2,1)} %get-tuple-element.7.back4), custom_call_target="tpu_custom_call" | custom-call | tf_op jit(solution)/shard_map/pallas_call | solution.py:623

commit v5 on v4

--- a/solution.py
+++ b/solution.py
@@ -453,9 +453,7 @@
 
     def next_block(c, sem):
         x2[block(c)] = finish(0, x0, c)
-        to_grid(x2, block(c))
         hel_start(1, x2, block(c), sem)
-        total[block(c)] = from_grid(block(c))
 
     next_block(me, 0)
 
@@ -464,7 +462,7 @@
         old_copy(i).wait_recv()
         next_block(source(i), n - shift(i))
 
-    total[...] += radial(x2)
+    multiply(x2)
     hel_arrived(1, x2)
 
     def make_out3(i):

time: 126 us -> 117 us (0.929)
  Pallas kernels: 125 us -> 116 us
    pallas_call x1, Pallas kernels: 122 us -> 113 us  [one_vibration(): pl.pallas_call(functools.partial(packet_kernel, n, hels), out_shape=(back...]
where the time goes in v5:
time: 117 us
  Pallas kernels  116 us (99%)
    pallas_call x1, Pallas kernels, one_vibration(): pl.pallas_call(functools.partial(packet_kernel, n, hels), out_shape=(back...  113 us
    pallas_call x1, Pallas kernels, one_vibration(): pl.pallas_call(functools.partial(place_kernel, n), out_shape=(flat, flat)...  3.24 us

profile of v5, /device:TPU:11, one launch (start us, length us, event | category | flops | bytes accessed | tf_op | source)
XLA Modules:
  0.0 117.0 jit_solution(17684201265699299828)
XLA Ops:
  0.6 113.1 %shard_map.95 = (bf16[8,64,1024]{2,1,0:T(8,128)(2,1)}, bf16[8,64,1024]{2,1,0:T(8,128)(2,1)}) custom-call(f32[512,1024]{1,0:T(8,128)} %bitcast.7, f32[512,1024]{1,0:T(8,128)} %bitcast.8, bf16[512,512]{1,0:T(8,128)(2,1)} %kinetic.1, bf16[1024,1024]{1,0:T(8,128)(2,1)} %bitcast.9, bf16[64,8,1024]{2,1,0:T(8,128)(2,1)} %potential.1, bf16[1,1024]{1,0:T(2,128)(2,1)} %coupling.1, ...), custom_call_target="tpu_custom_call" | custom-call | tf_op jit(solution)/shard_map/pallas_call | solution.py:565
  113.8 3.2 %shard_map.96 = (f32[512,1024]{1,0:T(8,128)}, f32[512,1024]{1,0:T(8,128)}) custom-call(bf16[8,64,1024]{2,1,0:T(8,128)(2,1)} %get-tuple-element.6.back3, bf16[8,64,1024]{2,1,0:T(8,128)(2,1)} %get-tuple-element.7.back4), custom_call_target="tpu_custom_call" | custom-call | tf_op jit(solution)/shard_map/pallas_call | solution.py:621
